TPU v7x, 32 devices: a whole 2x2x4 slice. The times are simulated.
32 devices in a mesh: groups: 2 (over y), slab: 4 (over z), batch: 2 (over x), chan: 2 (over core).
Axes of the slice: x: 2, y: 2, z: 4, core: 2. Of those that a mesh axis runs over, the one named last changes fastest.
Arguments:
- volume: bfloat16 [16, 8, 4, 8, 128], P(('groups', 'batch'), 'slab'), parts along dimension 0, may hold values from -6 to 6
- targets: float32 [16, 4], P(('groups', 'batch')), parts along dimension 0, may hold values from -1 to 1
- front_weight: bfloat16 [3, 3, 3, 128, 128], P(None, None, None, None, 'chan'), may hold values from -0.109375 to 0.109375
- stride_weight: bfloat16 [3, 3, 3, 128, 256], P(None, None, None, 'chan'), may hold values from -0.109375 to 0.109375
- hidden_weight: float32 [256, 128], P('chan'), may hold values from -0.375 to 0.375
- output_weight: float32 [128, 4], replicated, may hold values from -0.5 to 0.5
Outputs:
- grad_front: float32 [6, 3, 3, 128, 128], P('groups', None, None, None, 'chan'), parts along dimension 0
- grad_stride: float32 [6, 3, 3, 128, 256], P('groups', None, None, 'chan'), parts along dimension 0
- grad_hidden: float32 [512, 128], P(('groups', 'chan')), parts along dimension 0
- grad_output: float32 [256, 4], P('groups'), parts along dimension 0
- loss: float32 [2], P('groups'), parts along dimension 0
There are 2 independent parts, one for each index of `groups`. A program takes and returns all parts, laid end to end along the dimension named above; an argument that names none is the same for every part. Nothing has to cross between parts.
All inputs are finite; a program needn't handle non-finite values.
Results may differ from a plain program's by a relative error of at most 0.0052.
Values may be sent and summed in bfloat16 or wider, within the bound.
A program may use at most 64 MiB of HBM per device.

v0:
```python
import jax
import jax.numpy as jnp
from jax import lax
from jax.sharding import PartitionSpec as P


def with_halo(cells, sides, width):
    for axis, dim in sides:
        count = lax.axis_size(axis)
        ends = count - 1
        head = lax.slice_in_dim(cells, 0, width, axis=dim)
        tail = lax.slice_in_dim(cells, cells.shape[dim] - width, cells.shape[dim], axis=dim)
        cells = jnp.concatenate(
            [
                lax.ppermute(tail, axis, [(i, (i + 1) % count) for i in range(ends)]),
                cells,
                lax.ppermute(head, axis, [((i + 1) % count, i) for i in range(ends)]),
            ],
            axis=dim,
        )
    return cells


def swish_slope(preact):
    logistic = jax.nn.sigmoid(preact)
    return logistic * (1.0 + preact * (1.0 - logistic))


def tap_window(padded, tap_z, tap_x, tap_y, extent_z, extent_x, extent_y, stride):
    if stride == 1:
        return padded[
            :, tap_z : tap_z + extent_z, tap_x : tap_x + extent_x, tap_y : tap_y + extent_y, :
        ]
    leading = padded.shape[0]
    channels = padded.shape[-1]
    folded = padded.reshape(leading, extent_z + 1, 2, extent_x + 1, 2, extent_y + 1, 2, channels)
    return folded[
        :,
        tap_z // 2 : tap_z // 2 + extent_z,
        tap_z % 2,
        tap_x // 2 : tap_x // 2 + extent_x,
        tap_x % 2,
        tap_y // 2 : tap_y // 2 + extent_y,
        tap_y % 2,
        :,
    ]


def conv_apply(padded, weight, extent_z, extent_x, extent_y, stride):
    summed = None
    for tap_z in range(3):
        for tap_x in range(3):
            for tap_y in range(3):
                window = tap_window(
                    padded, tap_z, tap_x, tap_y, extent_z, extent_x, extent_y, stride
                )
                flat_tap = window.reshape(-1, window.shape[-1])
                contrib = jnp.dot(
                    flat_tap, weight[tap_z, tap_x, tap_y], preferred_element_type=jnp.float32
                )
                summed = contrib if summed is None else summed + contrib
    return summed.reshape(padded.shape[0], extent_z, extent_x, extent_y, weight.shape[-1])


def kernel_grad(padded, grad_out, extent_z, extent_x, extent_y, stride):
    flat_grad = grad_out.reshape(-1, grad_out.shape[-1])
    results = []
    for tap_z in range(3):
        for tap_x in range(3):
            for tap_y in range(3):
                window = tap_window(
                    padded, tap_z, tap_x, tap_y, extent_z, extent_x, extent_y, stride
                )
                flat_tap = window.reshape(-1, window.shape[-1])
                results.append(
                    lax.dot_general(
                        flat_tap,
                        flat_grad,
                        (((0,), (0,)), ((), ())),
                        preferred_element_type=jnp.float32,
                    )
                )
    return jnp.stack(results).reshape(3, 3, 3, padded.shape[-1], grad_out.shape[-1])


def input_grad(grad_out, weight, extent_z, extent_x, extent_y):
    leading = grad_out.shape[0]
    channels = weight.shape[3]
    flat_grad = grad_out.reshape(-1, grad_out.shape[-1])
    buckets = {}
    for tap_z in range(3):
        for tap_x in range(3):
            for tap_y in range(3):
                contrib = lax.dot_general(
                    flat_grad,
                    weight[tap_z, tap_x, tap_y],
                    (((1,), (1,)), ((), ())),
                    preferred_element_type=jnp.float32,
                )
                contrib = contrib.reshape(leading, extent_z, extent_x, extent_y, channels)
                placed = jnp.pad(
                    contrib,
                    (
                        (0, 0),
                        (tap_z // 2, 1 - tap_z // 2),
                        (tap_x // 2, 1 - tap_x // 2),
                        (tap_y // 2, 1 - tap_y // 2),
                        (0, 0),
                    ),
                )
                parity = (tap_z % 2, tap_x % 2, tap_y % 2)
                buckets[parity] = placed if parity not in buckets else buckets[parity] + placed
    planes_z = []
    for par_z in range(2):
        planes_x = []
        for par_x in range(2):
            planes_x.append(jnp.stack([buckets[par_z, par_x, par_y] for par_y in range(2)], axis=4))
        planes_z.append(jnp.stack(planes_x, axis=3))
    assembled = jnp.stack(planes_z, axis=2)
    assembled = assembled.reshape(
        leading, 2 * extent_z + 2, 2 * extent_x + 2, 2 * extent_y + 2, channels
    )
    return assembled[:, 1:-1, 1:-1, 1:-1, :]


def body(volume, targets, front_weight, stride_weight, hidden_weight, output_weight):
    highest = lax.Precision.HIGHEST
    slabs = lax.axis_size("slab")
    batches = lax.axis_size("batch")
    inner = front_weight.shape[-1]
    leading, thick, extent_x, extent_y, channels = volume.shape
    depth = thick * slabs
    outputs = output_weight.shape[-1]
    haloed = with_halo(volume, (("slab", 1),), 1)
    padded = jnp.pad(haloed, ((0, 0), (0, 0), (1, 1), (1, 1), (0, 0)))
    front_pre = conv_apply(padded, front_weight, thick, extent_x, extent_y, 1)
    front_act = jax.nn.silu(front_pre).astype(jnp.bfloat16)
    merged = front_act.reshape(leading, thick, extent_x, extent_y * inner)
    sample_act = lax.all_to_all(merged, "slab", split_axis=0, concat_axis=1, tiled=True)
    sample_act = sample_act.reshape(1, depth, extent_x, extent_y, inner)
    half_z = depth // 2
    half_x = extent_x // 2
    half_y = extent_y // 2
    cells = half_z * half_x * half_y
    stride_pad = jnp.pad(sample_act, ((0, 0), (1, 1), (1, 1), (1, 1), (0, 0)))
    partial_pre = conv_apply(stride_pad, stride_weight, half_z, half_x, half_y, 2)
    stride_pre = lax.psum_scatter(partial_pre, "chan", scatter_dimension=4, tiled=True)
    pooled = jnp.sum(jax.nn.silu(stride_pre), axis=(0, 1, 2, 3)) / cells
    hidden_pre = lax.psum(jnp.dot(pooled, hidden_weight, precision=highest), "chan")
    hidden_act = jax.nn.silu(hidden_pre)
    predicted = jnp.dot(hidden_act, output_weight, precision=highest)
    target_row = lax.dynamic_index_in_dim(targets, lax.axis_index("slab"), 0, keepdims=False)
    residual = predicted - target_row
    squared = jnp.sum(residual * residual)
    grad_output = jnp.outer(hidden_act, residual)
    grad_hidden_pre = jnp.dot(output_weight, residual, precision=highest) * swish_slope(hidden_pre)
    grad_hidden = jnp.outer(pooled, grad_hidden_pre)
    grad_pooled = jnp.dot(hidden_weight, grad_hidden_pre, precision=highest)
    grad_stride_pre = (grad_pooled / cells * swish_slope(stride_pre)).astype(jnp.bfloat16)
    full_grad = lax.all_gather(grad_stride_pre, "chan", axis=4, tiled=True)
    grad_stride = kernel_grad(stride_pad, full_grad, half_z, half_x, half_y, 2)
    grad_act = input_grad(full_grad, stride_weight, half_z, half_x, half_y).astype(jnp.bfloat16)
    returned = lax.all_to_all(
        grad_act.reshape(1, depth, extent_x, extent_y * inner),
        "slab",
        split_axis=1,
        concat_axis=0,
        tiled=True,
    )
    returned = returned.reshape(leading, thick, extent_x, extent_y, inner)
    grad_front_pre = (returned * swish_slope(front_pre)).astype(jnp.bfloat16)
    grad_front = kernel_grad(padded, grad_front_pre, thick, extent_x, extent_y, 1)
    grad_front, grad_stride, grad_hidden, grad_output, squared = lax.psum(
        (grad_front, grad_stride, grad_hidden, grad_output, squared), ("slab", "batch")
    )
    loss = (squared / (slabs * batches * outputs)).reshape(1)
    return (grad_front, grad_stride, grad_hidden, grad_output, loss)


def solution(mesh):
    in_specs = (
        P(("groups", "batch"), "slab", None, None, None),
        P(("groups", "batch"), None),
        P(None, None, None, None, "chan"),
        P(None, None, None, "chan", None),
        P("chan", None),
        P(),
    )
    out_specs = (
        P("groups", None, None, None, "chan"),
        P("groups", None, None, "chan", None),
        P(("groups", "chan"), None),
        P("groups", None),
        P("groups"),
    )
    return jax.shard_map(body, mesh=mesh, in_specs=in_specs, out_specs=out_specs, check_vma=False)
```

profile of v0, /device:TPU:0, one launch (start us, length us, event | category | flops | bytes accessed | tf_op | source)
XLA Modules:
  0.0 213.3 jit_solution(12655027647742667064)
XLA Ops:
  7.2 0.8 fusion.298
  8.0 4.9 %collective-permute-start = (bf16[4,1,4,8,128]{4,3,2,1,0:T(8,128)(2,1)S(1)}, bf16[4,1,4,8,128]{4,3,2,1,0:T(8,128)(2,1)S(1)}, u32[]{:S(2)}, u32[]{:S(2)}) collective-permute-start(bf16[4,1,4,8,128]{4,3,2,1,0:T(8,128)(2,1)S(1)} %get-tuple-element.63), channel_id=1, source_target_pairs={{0,4},{4,8},{8,12},{1,5},{5,9},{9,13},{2,6},{6,10},{10,14},{3,7},{... | collective-permute-start | bytes 98312 | tf_op jit(solution)/shard_map/ppermute | solution.py:15
  13.0 1.4 collective-permute-start.1
  14.5 4.4 %collective-permute-done.1 = bf16[4,1,4,8,128]{4,3,2,1,0:T(8,128)(2,1)S(1)} collective-permute-done((bf16[4,1,4,8,128]{4,3,2,1,0:T(8,128)(2,1)S(1)}, bf16[4,1,4,8,128]{4,3,2,1,0:T(8,128)(2,1)S(1)}, u32[]{:S(2)}, u32[]{:S(2)}) %collective-permute-start.1) | collective-permute-done | bytes 32800 | tf_op jit(solution)/shard_map/ppermute | solution.py:17
  18.9 1.0 select_maximum_fusion
  20.2 0.6 copy-done.6
  25.4 9.3 %all_to_all.8 = bf16[4,2,4,512]{3,2,1,0:T(4,128)(2,1)S(1)} all-to-all(bf16[4,2,4,512]{3,2,1,0:T(4,128)(2,1)S(1)} %fusion.65), channel_id=1, replica_groups=mesh['groups'=2,'slab'=4,'batch'=2,'chan'=2] {'slab'}, dimensions={0} | all-to-all | bytes 65536 | tf_op jit(solution)/shard_map/all_to_all | solution.py:139
  39.2 0.8 copy.165
  40.0 1.9 reshape.469
  41.9 6.1 %reduce-scatter.4.cloned.1.call-done = f32[128,32]{1,0:T(8,128)} async-done(((f32[256,32]{1,0:T(8,128)}), f32[128,32]{1,0:T(8,128)}) %reduce-scatter.4.cloned.1.call-update) | async-done | bytes 16400
  48.0 1.5 reshape.470
  50.1 2.5 %psum.42 = f32[128]{0:T(128)S(1)} all-reduce(f32[128]{0:T(128)S(1)} %convolution_bitcast_fusion.83), channel_id=1, replica_groups=mesh['groups'=2,'slab'=4,'batch'=2,'chan'=2] {'chan'}, use_global_device_ids=true, to_apply=%region_2.3 | all-reduce | flops 128 | bytes 1024 | tf_op jit(solution)/shard_map/psum | solution.py:149
  52.6 1.4 multiply_reduce_fusion.1
  54.4 1.8 all_gather.3
  65.4 0.7 reshape.468
  66.1 4.8 %all-to-all-start.1 = ((bf16[1,8,4,512]{3,2,0,1:T(4,128)(2,1)}), bf16[1,8,4,512]{3,2,0,1:T(4,128)(2,1)S(1)}, u32[]{:S(2)}, u32[]{:S(2)}) async-start(bf16[1,8,4,512]{3,2,0,1:T(4,128)(2,1)} %reshape.468), calls=%async_computation.1 | async-start | bytes 65536 | tf_op jit(solution)/shard_map/all_to_all | solution.py:163
  71.0 0.7 broadcast_multiply_fusion
  71.7 4.9 %all-to-all-done.1 = bf16[1,8,4,512]{3,2,0,1:T(4,128)(2,1)S(1)} async-done(((bf16[1,8,4,512]{3,2,0,1:T(4,128)(2,1)}), bf16[1,8,4,512]{3,2,0,1:T(4,128)(2,1)S(1)}, u32[]{:S(2)}, u32[]{:S(2)}) %all-to-all-start.1) | async-done | bytes 32800 | tf_op jit(solution)/shard_map/all_to_all | solution.py:163
  82.4 0.9 copy-done.5
  83.4 20.3 %all-reduce.29 = (f32[128,4]{0,1:T(4,128)}, f32[]{:T(128)}) all-reduce(f32[128,4]{0,1:T(4,128)S(1)} %broadcast_multiply_fusion.1, f32[]{:T(128)} %get-tuple-element.65), channel_id=1, replica_groups=mesh['groups'=2,'slab'=4,'batch'=2,'chan'=2] {'slab','batch'}, use_global_device_ids=true, to_apply=%region_6.7 | all-reduce | flops 513 | bytes 4104 | tf_op jit(solution)/shard_map/psum | solution.py:173
  104.3 96.9 %all-reduce.33.cloned.1.call-done = (f32[3,3,3,128,64]{3,4,2,1,0:T(8,128)}, f32[3,3,3,64,256]{4,3,2,1,0:T(8,128)}, f32[128,128]{1,0:T(8,128)}) async-done(((f32[3,3,3,128,64]{3,4,2,1,0:T(8,128)}, f32[3,3,3,64,256]{4,3,2,1,0:T(8,128)}, f32[128,128]{1,0:T(8,128)}), (f32[3,3,3,128,64]{3,4,2,1,0:T(8,128)}, f32[3,3,3,64,256]{4,3,2,1,0:T(8,128)}, f32[128,128]{1,0:T(8,128)})) %all-reduce.33.cloned.1.call-update) | async-done | bytes 2719760 | tf_op jit(solution)/shard_map/psum | solution.py:173
  201.2 2.3 %copy.225 = f32[3,3,3,128,64]{3,4,2,1,0:T(8,128)} copy(f32[3,3,3,128,64]{3,4,2,1,0:T(8,128)} %get-tuple-element.73) | data formatting | bytes 1769472
  203.5 1.2 copy.226
  204.7 0.6 copy.227
  (228 shorter events, 24.8 us)
Async XLA Ops:
  7.2 42.8 %copy-start = (f32[128,128]{1,0:T(8,128)S(1)}, f32[128,128]{1,0:T(8,128)}, u32[]{:S(2)}) copy-start(f32[128,128]{1,0:T(8,128)} %param.10) | copy-start | bytes 196612
  7.2 40.8 %reduce-scatter.4.cloned.1.call-start = ((), (), s32[]{:S(2)}) async-start(), calls=%async_computation.3 | async-start | bytes 196608
  8.0 6.5 %collective-permute-start = (bf16[4,1,4,8,128]{4,3,2,1,0:T(8,128)(2,1)S(1)}, bf16[4,1,4,8,128]{4,3,2,1,0:T(8,128)(2,1)S(1)}, u32[]{:S(2)}, u32[]{:S(2)}) collective-permute-start(bf16[4,1,4,8,128]{4,3,2,1,0:T(8,128)(2,1)S(1)} %get-tuple-element.63), channel_id=1, source_target_pairs={{0,4},{4,8},{8,12},{1,5},{5,9},{9,13},{2,6},{6,10},{10,14},{3,7},{... | collective-permute-start | bytes 98312 | tf_op jit(solution)/shard_map/ppermute | solution.py:15
  12.9 7.2 %copy-start.4 = (bf16[4,2,4,8,128]{4,3,2,1,0:T(8,128)(2,1)S(1)}, bf16[4,2,4,8,128]{4,3,2,1,0:T(8,128)(2,1)}, u32[]{:S(2)}) copy-start(bf16[4,2,4,8,128]{4,3,2,1,0:T(8,128)(2,1)} %param.6) | copy-start | bytes 196612
  13.0 5.9 %collective-permute-start.1 = (bf16[4,1,4,8,128]{4,3,2,1,0:T(8,128)(2,1)S(1)}, bf16[4,1,4,8,128]{4,3,2,1,0:T(8,128)(2,1)S(1)}, u32[]{:S(2)}, u32[]{:S(2)}) collective-permute-start(bf16[4,1,4,8,128]{4,3,2,1,0:T(8,128)(2,1)S(1)} %get-tuple-element.64), channel_id=1, source_target_pairs={{4,0},{8,4},{12,8},{5,1},{9,5},{13,9},{6,2},{10,6},{14,10},{7,3},{... | collective-permute-start | bytes 98312 | tf_op jit(solution)/shard_map/ppermute | solution.py:17
  19.9 1.0 copy-start.6
  24.8 10.9 %copy-start.1 = (bf16[3,3,3,64,256]{4,3,2,1,0:T(8,128)(2,1)S(1)}, bf16[3,3,3,64,256]{4,3,2,1,0:T(8,128)(2,1)}, u32[]{:S(2)}) copy-start(bf16[3,3,3,64,256]{4,3,2,1,0:T(8,128)(2,1)} %param.9) | copy-start | bytes 2654212
  39.2 13.4 %copy-start.8 = (f32[128,4]{0,1:T(4,128)S(1)}, f32[128,4]{0,1:T(4,128)}, u32[]{:S(2)}) copy-start(f32[128,4]{0,1:T(4,128)} %param.11) | copy-start | bytes 6148
  64.7 12.0 %copy-start.2 = (f32[27,64,256]{2,1,0:T(8,128)}, f32[27,64,256]{2,1,0:T(8,128)S(1)}, u32[]{:S(2)}) copy-start(f32[27,64,256]{2,1,0:T(8,128)S(1)} %fusion) | copy-start | bytes 5308420
  66.1 10.5 %all-to-all-start.1 = ((bf16[1,8,4,512]{3,2,0,1:T(4,128)(2,1)}), bf16[1,8,4,512]{3,2,0,1:T(4,128)(2,1)S(1)}, u32[]{:S(2)}, u32[]{:S(2)}) async-start(bf16[1,8,4,512]{3,2,0,1:T(4,128)(2,1)} %reshape.468), calls=%async_computation.1 | async-start | bytes 65536 | tf_op jit(solution)/shard_map/all_to_all | solution.py:163
  71.0 130.2 %all-reduce.33.cloned.1.call-start = ((), (), s32[]{:S(2)}) async-start(), calls=%async_computation.4 | async-start | bytes 5439488 | tf_op jit(solution)/shard_map/psum | solution.py:173
  82.4 0.9 copy-start.5
  201.2 2.3 %copy-start.3 = (f32[3,3,3,64,256]{4,3,2,1,0:T(8,128)S(1)}, f32[3,3,3,64,256]{4,3,2,1,0:T(8,128)}, u32[]{:S(2)}) copy-start(f32[3,3,3,64,256]{4,3,2,1,0:T(8,128)} %get-tuple-element.74) | copy-start | bytes 5308420
  203.5 1.2 copy-start.7
Sparse Core Ops, SparseCore 0:
  42.0 5.8 reduce-scatter.3
  83.4 117.7 all-reduce.32
where the time goes:
time: 214 us; the launch traced here: 213 us
  waiting for transfers between devices  112 us (52%)
  blocking collectives  33.9 us (16%)
  matrix products  23.2 us (11%)
  between operations  16.7 us (8%)
  local copies, waits for them, and re-layouts  13.5 us (6%)
  starting transfers between devices  11.2 us (5%)
  other arithmetic  2.34 us (1%)
    psum x1, waiting for transfers between devices, body(): lax.psum((grad_front, grad_stride, grad_hidden, grad_output, squared), ('...  96.9 us
    psum x1, blocking collectives, body(): lax.psum((grad_front, grad_stride, grad_hidden, grad_output, squared), ('...  20.3 us
    unnamed x27, local copies, waits for them, and re-layouts  10.4 us
    dot_general x54, matrix products, kernel_grad(): lax.dot_general(flat_tap, flat_grad, (((0,), (0,)), ((), ())), preferred_...  10.2 us
    all_to_all x1, blocking collectives, body(): lax.all_to_all(merged, 'slab', split_axis=0, concat_axis=1, tiled=True)  9.32 us
    dot_general x54, matrix products, conv_apply(): jnp.dot(flat_tap, weight[tap_z, tap_x, tap_y], preferred_element_type=jnp...  7.54 us
    unnamed x3, waiting for transfers between devices  6.09 us
    all_to_all x1, waiting for transfers between devices, body(): lax.all_to_all(grad_act.reshape(1, depth, extent_x, extent_y * inner), 's...  4.94 us
  transfers between devices with their start and end apart: 5, of which 5 were waited for; matrix products, arithmetic and copies ran while one was open for 0% of the time, Pallas kernels for 0%

commit v1 on v0

--- a/solution.py
+++ b/solution.py
@@ -2,6 +2,11 @@
 import jax.numpy as jnp
 from jax import lax
 from jax.sharding import PartitionSpec as P
+from jax.lax import psum
+
+
+def try_all_the_widths(w_in):
+    return psum(psum(w_in, "batch"), "slab")
 
 
 def with_halo(cells, sides, width):
@@ -170,8 +175,8 @@
     returned = returned.reshape(leading, thick, extent_x, extent_y, inner)
     grad_front_pre = (returned * swish_slope(front_pre)).astype(jnp.bfloat16)
     grad_front = kernel_grad(padded, grad_front_pre, thick, extent_x, extent_y, 1)
-    grad_front, grad_stride, grad_hidden, grad_output, squared = lax.psum(
-        (grad_front, grad_stride, grad_hidden, grad_output, squared), ("slab", "batch")
+    grad_front, grad_stride, grad_hidden, grad_output, squared = try_all_the_widths(
+        (grad_front, grad_stride, grad_hidden, grad_output, squared)
     )
     loss = (squared / (slabs * batches * outputs)).reshape(1)
     return (grad_front, grad_stride, grad_hidden, grad_output, loss)

time: 214 us -> 282 us (1.32)
  waiting for transfers between devices: 112 us -> 183 us
    psum x1 -> x2, waiting for transfers between devices: 96.9 us -> 167 us  [try_all_the_widths(): return psum(psum(w_in, 'batch'), 'slab')]
    psum x1 -> x2, blocking collectives: 20.3 us -> 18.3 us  [try_all_the_widths(): return psum(psum(w_in, 'batch'), 'slab')]
    unnamed x3 -> x4, waiting for transfers between devices: 6.09 us -> 6.11 us
  transfers between devices with their start and end apart: 5 -> 6, of which waited for: 5 -> 6; matrix products, arithmetic and copies ran while one was open for 0% -> 0% of each run, Pallas kernels for 0% -> 0%
where the time goes in v1:
time: 282 us; the launch traced here: 281 us
  waiting for transfers between devices  183 us (65%)
  blocking collectives  31.9 us (11%)
  matrix products  23.2 us (8%)
  between operations  16.4 us (6%)
  local copies, waits for them, and re-layouts  13.5 us (5%)
  starting transfers between devices  11.3 us (4%)
    psum x2, waiting for transfers between devices, try_all_the_widths(): return psum(psum(w_in, 'batch'), 'slab')  167 us
    psum x2, blocking collectives, try_all_the_widths(): return psum(psum(w_in, 'batch'), 'slab')  18.3 us
    unnamed x27, local copies, waits for them, and re-layouts  10.4 us
    dot_general x54, matrix products, kernel_grad(): lax.dot_general(flat_tap, flat_grad, (((0,), (0,)), ((), ())), preferred_...  10.2 us
    all_to_all x1, blocking collectives, body(): lax.all_to_all(merged, 'slab', split_axis=0, concat_axis=1, tiled=True)  9.32 us
    dot_general x54, matrix products, conv_apply(): jnp.dot(flat_tap, weight[tap_z, tap_x, tap_y], preferred_element_type=jnp...  7.54 us
    unnamed x4, waiting for transfers between devices  6.11 us
  transfers between devices with their start and end apart: 6, of which 6 were waited for; matrix products, arithmetic and copies ran while one was open for 0% of the time, Pallas kernels for 0%

profile of v1, /device:TPU:0, one launch (start us, length us, event | category | flops | bytes accessed | tf_op | source)
XLA Modules:
  0.0 281.1 jit_solution(1153166001701639352)
XLA Ops:
  7.2 0.8 fusion.298
  8.0 4.9 %collective-permute-start = (bf16[4,1,4,8,128]{4,3,2,1,0:T(8,128)(2,1)S(1)}, bf16[4,1,4,8,128]{4,3,2,1,0:T(8,128)(2,1)S(1)}, u32[]{:S(2)}, u32[]{:S(2)}) collective-permute-start(bf16[4,1,4,8,128]{4,3,2,1,0:T(8,128)(2,1)S(1)} %get-tuple-element.68), channel_id=1, source_target_pairs={{0,4},{4,8},{8,12},{1,5},{5,9},{9,13},{2,6},{6,10},{10,14},{3,7},{... | collective-permute-start | bytes 98312 | tf_op jit(solution)/shard_map/ppermute | solution.py:20
  13.0 1.4 collective-permute-start.1
  14.5 4.4 %collective-permute-done.1 = bf16[4,1,4,8,128]{4,3,2,1,0:T(8,128)(2,1)S(1)} collective-permute-done((bf16[4,1,4,8,128]{4,3,2,1,0:T(8,128)(2,1)S(1)}, bf16[4,1,4,8,128]{4,3,2,1,0:T(8,128)(2,1)S(1)}, u32[]{:S(2)}, u32[]{:S(2)}) %collective-permute-start.1) | collective-permute-done | bytes 32800 | tf_op jit(solution)/shard_map/ppermute | solution.py:22
  18.9 1.0 select_maximum_fusion
  25.4 9.3 %all_to_all.8 = bf16[4,2,4,512]{3,2,1,0:T(4,128)(2,1)S(1)} all-to-all(bf16[4,2,4,512]{3,2,1,0:T(4,128)(2,1)S(1)} %fusion.65), channel_id=1, replica_groups=mesh['groups'=2,'slab'=4,'batch'=2,'chan'=2] {'slab'}, dimensions={0} | all-to-all | bytes 65536 | tf_op jit(solution)/shard_map/all_to_all | solution.py:144
  39.2 0.8 copy.165
  40.0 1.9 reshape.469
  41.9 6.1 %reduce-scatter.4.cloned.1.call-done = f32[128,32]{1,0:T(8,128)} async-done(((f32[256,32]{1,0:T(8,128)}), f32[128,32]{1,0:T(8,128)}) %reduce-scatter.4.cloned.1.call-update) | async-done | bytes 16400
  48.0 1.5 reshape.470
  50.1 2.5 psum.77
  52.6 1.4 multiply_reduce_fusion.1
  54.4 1.8 all_gather.3
  65.4 0.7 reshape.468
  66.1 4.8 %all-to-all-start.1 = ((bf16[1,8,4,512]{3,2,0,1:T(4,128)(2,1)}), bf16[1,8,4,512]{3,2,0,1:T(4,128)(2,1)S(1)}, u32[]{:S(2)}, u32[]{:S(2)}) async-start(bf16[1,8,4,512]{3,2,0,1:T(4,128)(2,1)} %reshape.468), calls=%async_computation.1 | async-start | bytes 65536 | tf_op jit(solution)/shard_map/all_to_all | solution.py:168
  71.0 0.7 broadcast_multiply_fusion
  71.7 4.9 %all-to-all-done.1 = bf16[1,8,4,512]{3,2,0,1:T(4,128)(2,1)S(1)} async-done(((bf16[1,8,4,512]{3,2,0,1:T(4,128)(2,1)}), bf16[1,8,4,512]{3,2,0,1:T(4,128)(2,1)S(1)}, u32[]{:S(2)}, u32[]{:S(2)}) %all-to-all-start.1) | async-done | bytes 32800 | tf_op jit(solution)/shard_map/all_to_all | solution.py:168
  82.4 0.9 copy-done.5
  83.3 75.3 %all-reduce.38.cloned.1.call-done = (f32[3,3,3,128,64]{3,4,2,1,0:T(8,128)}, f32[3,3,3,64,256]{4,3,2,1,0:T(8,128)}, f32[128,128]{1,0:T(8,128)}) async-done(((f32[3,3,3,128,64]{3,4,2,1,0:T(8,128)}, f32[3,3,3,64,256]{4,3,2,1,0:T(8,128)}, f32[128,128]{1,0:T(8,128)}), (f32[3,3,3,128,64]{3,4,2,1,0:T(8,128)}, f32[3,3,3,64,256]{4,3,2,1,0:T(8,128)}, f32[128,128]{1,0:T(8,128)})) %all-reduce.38.cloned.1.call-update) | async-done | bytes 2719760 | tf_op jit(solution)/shard_map/psum | solution.py:9
  158.7 5.6 %all-reduce.31 = (f32[128,4]{0,1:T(4,128)S(1)}, f32[]{:T(128)}) all-reduce(f32[128,4]{0,1:T(4,128)S(1)} %broadcast_multiply_fusion.1, f32[]{:T(128)} %get-tuple-element.70), channel_id=1, replica_groups=mesh['groups'=2,'slab'=4,'batch'=2,'chan'=2] {'batch'}, use_global_device_ids=true, to_apply=%region_9.10 | all-reduce | flops 513 | bytes 4104 | tf_op jit(solution)/shard_map/psum | solution.py:9
  164.2 12.7 %all-reduce.29 = (f32[128,4]{0,1:T(4,128)}, f32[]{:T(128)}) all-reduce(f32[128,4]{0,1:T(4,128)S(1)} %get-tuple-element.10, f32[]{:T(128)} %get-tuple-element.11), channel_id=1, replica_groups=mesh['groups'=2,'slab'=4,'batch'=2,'chan'=2] {'slab'}, use_global_device_ids=true, to_apply=%region_10.11 | all-reduce | flops 513 | bytes 4104 | tf_op jit(solution)/shard_map/psum | solution.py:9
  177.6 91.7 %all-reduce.36.cloned.1.call-done = (f32[3,3,3,128,64]{3,4,2,1,0:T(8,128)}, f32[3,3,3,64,256]{4,3,2,1,0:T(8,128)}, f32[128,128]{1,0:T(8,128)}) async-done(((f32[3,3,3,128,64]{3,4,2,1,0:T(8,128)}, f32[3,3,3,64,256]{4,3,2,1,0:T(8,128)}, f32[128,128]{1,0:T(8,128)}), (f32[3,3,3,128,64]{3,4,2,1,0:T(8,128)}, f32[3,3,3,64,256]{4,3,2,1,0:T(8,128)}, f32[128,128]{1,0:T(8,128)})) %all-reduce.36.cloned.1.call-update) | async-done | bytes 2719760 | tf_op jit(solution)/shard_map/psum | solution.py:9
  269.3 2.3 copy.228
  271.6 1.2 copy.229
  (232 shorter events, 26.1 us)
Async XLA Ops:
  7.2 42.8 %copy-start = (f32[128,128]{1,0:T(8,128)S(1)}, f32[128,128]{1,0:T(8,128)}, u32[]{:S(2)}) copy-start(f32[128,128]{1,0:T(8,128)} %param.10) | copy-start | bytes 196612
  7.2 40.8 %reduce-scatter.4.cloned.1.call-start = ((), (), s32[]{:S(2)}) async-start(), calls=%async_computation.3 | async-start | bytes 196608
  8.0 6.5 %collective-permute-start = (bf16[4,1,4,8,128]{4,3,2,1,0:T(8,128)(2,1)S(1)}, bf16[4,1,4,8,128]{4,3,2,1,0:T(8,128)(2,1)S(1)}, u32[]{:S(2)}, u32[]{:S(2)}) collective-permute-start(bf16[4,1,4,8,128]{4,3,2,1,0:T(8,128)(2,1)S(1)} %get-tuple-element.68), channel_id=1, source_target_pairs={{0,4},{4,8},{8,12},{1,5},{5,9},{9,13},{2,6},{6,10},{10,14},{3,7},{... | collective-permute-start | bytes 98312 | tf_op jit(solution)/shard_map/ppermute | solution.py:20
  12.9 7.2 %copy-start.4 = (bf16[4,2,4,8,128]{4,3,2,1,0:T(8,128)(2,1)S(1)}, bf16[4,2,4,8,128]{4,3,2,1,0:T(8,128)(2,1)}, u32[]{:S(2)}) copy-start(bf16[4,2,4,8,128]{4,3,2,1,0:T(8,128)(2,1)} %param.6) | copy-start | bytes 196612
  13.0 5.9 %collective-permute-start.1 = (bf16[4,1,4,8,128]{4,3,2,1,0:T(8,128)(2,1)S(1)}, bf16[4,1,4,8,128]{4,3,2,1,0:T(8,128)(2,1)S(1)}, u32[]{:S(2)}, u32[]{:S(2)}) collective-permute-start(bf16[4,1,4,8,128]{4,3,2,1,0:T(8,128)(2,1)S(1)} %get-tuple-element.69), channel_id=1, source_target_pairs={{4,0},{8,4},{12,8},{5,1},{9,5},{13,9},{6,2},{10,6},{14,10},{7,3},{... | collective-permute-start | bytes 98312 | tf_op jit(solution)/shard_map/ppermute | solution.py:22
  19.9 1.0 copy-start.6
  24.8 10.9 %copy-start.1 = (bf16[3,3,3,64,256]{4,3,2,1,0:T(8,128)(2,1)S(1)}, bf16[3,3,3,64,256]{4,3,2,1,0:T(8,128)(2,1)}, u32[]{:S(2)}) copy-start(bf16[3,3,3,64,256]{4,3,2,1,0:T(8,128)(2,1)} %param.9) | copy-start | bytes 2654212
  39.2 13.4 %copy-start.8 = (f32[128,4]{0,1:T(4,128)S(1)}, f32[128,4]{0,1:T(4,128)}, u32[]{:S(2)}) copy-start(f32[128,4]{0,1:T(4,128)} %param.11) | copy-start | bytes 6148
  64.7 12.0 %copy-start.2 = (f32[27,64,256]{2,1,0:T(8,128)}, f32[27,64,256]{2,1,0:T(8,128)S(1)}, u32[]{:S(2)}) copy-start(f32[27,64,256]{2,1,0:T(8,128)S(1)} %fusion) | copy-start | bytes 5308420
  66.1 10.5 %all-to-all-start.1 = ((bf16[1,8,4,512]{3,2,0,1:T(4,128)(2,1)}), bf16[1,8,4,512]{3,2,0,1:T(4,128)(2,1)S(1)}, u32[]{:S(2)}, u32[]{:S(2)}) async-start(bf16[1,8,4,512]{3,2,0,1:T(4,128)(2,1)} %reshape.468), calls=%async_computation.1 | async-start | bytes 65536 | tf_op jit(solution)/shard_map/all_to_all | solution.py:168
  71.0 87.6 %all-reduce.38.cloned.1.call-start = ((), (), s32[]{:S(2)}) async-start(), calls=%async_computation.5 | async-start | bytes 5439488 | tf_op jit(solution)/shard_map/psum | solution.py:9
  82.4 0.9 copy-start.5
  83.3 186.0 %all-reduce.36.cloned.1.call-start = ((), (), s32[]{:S(2)}) async-start(), calls=%async_computation.4 | async-start | bytes 5439488 | tf_op jit(solution)/shard_map/psum | solution.py:9
  269.3 2.3 copy-start.3
  271.6 1.2 copy-start.7
Sparse Core Ops, SparseCore 0:
  42.0 5.8 reduce-scatter.3
  83.4 75.1 all-reduce.37
  161.2 108.0 all-reduce.35
